TPU v7x, 32 devices: a whole 2x2x4 slice. The times are simulated.
32 devices in a mesh: group: 2 (over y), shard: 16 (over z, x, core).
Axes of the slice: x: 2, y: 2, z: 4, core: 2. Of those that a mesh axis runs over, the one named last changes fastest.
Arguments:
- samples: bfloat16 [32, 8192], P('shard'), may hold values from -6 to 6
- factor_old: float32 [8192, 8192], P('shard', 'group'), as said below
- damping: float32 [1], replicated, may hold values from 0.1 to 1
- gradients: bfloat16 [2048, 8192], P('shard', 'group'), may hold values from -6 to 6
Outputs:
- swept_factor: float32 [8192, 8192], P('shard', 'group')
- update: bfloat16 [8192, 2048], P('shard', 'group')
Inputs may be any that keep to these rules, and one draw needn't show every extreme that they name: factor_old is symmetric and positive definite.
All inputs are finite; a program needn't handle non-finite values.
Results may differ from a plain program's by a relative error of at most 0.0049.
Values may be sent and summed in bfloat16 or wider, within the bound.
A program may use at most 128 MiB of HBM per device.

v0:
```python
import jax
import jax.numpy as jnp
from jax import lax
from jax.sharding import PartitionSpec as P

D = 8192
BLOCK = 128
PIVOTS = 2
ema_keep = 0.5


def spread(block, axis, holder):
    block = jnp.where(lax.axis_index(axis) == holder, block, jnp.zeros_like(block))
    return lax.psum(block, axis)


def solve_spd(pivot_block, right_side):
    lower_factor = jnp.linalg.cholesky(pivot_block)
    half_solved = lax.linalg.triangular_solve(lower_factor, right_side, left_side=True, lower=True)
    return lax.linalg.triangular_solve(
        lower_factor, half_solved, left_side=True, lower=True, transpose_a=True
    )


def on_device(samples, factor_old, damping, gradients):
    row_count, col_count = factor_old.shape
    shard_index = lax.axis_index("shard")
    group_index = lax.axis_index("group")
    row_first = shard_index * row_count
    col_first = group_index * col_count
    total_tokens = samples.shape[0] * lax.axis_size("shard")
    contract = (((0,), (0,)), ((), ()))
    token_piece = lax.all_gather(samples, "shard", axis=0, tiled=True)
    left_part = lax.dynamic_slice_in_dim(token_piece, row_first, row_count, 1)
    right_part = lax.dynamic_slice_in_dim(token_piece, col_first, col_count, 1)
    covariance = lax.dot_general(
        left_part, right_part, contract, preferred_element_type=jnp.float32
    )
    row_ids = lax.broadcasted_iota(jnp.int32, (row_count, col_count), 0) + row_first
    col_ids = lax.broadcasted_iota(jnp.int32, (row_count, col_count), 1) + col_first
    diagonal = jnp.where(row_ids == col_ids, damping[0], 0.0)
    factor = ema_keep * factor_old + (1.0 - ema_keep) * (covariance / total_tokens) + diagonal
    spacing = D // PIVOTS
    sel_rows = lax.broadcasted_iota(jnp.int32, (BLOCK, col_count), 0)
    sel_cols = lax.broadcasted_iota(jnp.int32, (BLOCK, col_count), 1) + col_first

    def sweep_once(sweep_step, matrix):
        first_index = (sweep_step * spacing).astype(jnp.int32)
        col_owner = first_index // col_count
        row_owner = first_index // row_count
        col_offset = first_index - col_owner * col_count
        row_offset = first_index - row_owner * row_count
        own_columns = lax.dynamic_slice_in_dim(matrix, col_offset, BLOCK, 1)
        column = spread(own_columns, "group", col_owner)
        own_rows = lax.dynamic_slice_in_dim(matrix, row_offset, BLOCK, 0)
        own_pivot = lax.dynamic_slice_in_dim(column, row_offset, BLOCK, 0)
        pivot_strip, pivot_block = (
            spread(own_rows, "shard", row_owner),
            spread(own_pivot, "shard", row_owner),
        )
        selector = jnp.where(sel_cols == sel_rows + first_index, 1.0, 0.0).astype(jnp.float32)
        factor_q = solve_spd(pivot_block, pivot_strip + selector)
        matrix = matrix - jnp.dot(
            column, factor_q, precision=lax.Precision.HIGHEST, preferred_element_type=jnp.float32
        )
        addition = jnp.where(shard_index == row_owner, factor_q, 0.0)
        block_rows = lax.dynamic_slice_in_dim(matrix, row_offset, BLOCK, 0) + addition
        return lax.dynamic_update_slice_in_dim(matrix, block_rows, row_offset, 0)

    swept_factor = lax.fori_loop(0, PIVOTS, sweep_once, factor)
    swept_half = swept_factor.astype(jnp.bfloat16)
    partial_terms = lax.dot_general(
        swept_half,
        lax.all_gather(gradients, "shard", axis=0, tiled=True),
        (((1,), (1,)), ((), ())),
        preferred_element_type=jnp.float32,
    )
    update = lax.psum_scatter(partial_terms, "group", scatter_dimension=1, tiled=True).astype(
        jnp.bfloat16
    )
    return (swept_factor, update)


def solution(mesh):
    return jax.shard_map(
        on_device,
        mesh=mesh,
        in_specs=(P("shard", None), P("shard", "group"), P(), P("shard", "group")),
        out_specs=(P("shard", "group"), P("shard", "group")),
        check_vma=False,
    )
```

profile of v0, /device:TPU:0, one launch (start us, length us, event | category | flops | bytes accessed | tf_op | source)
XLA Modules:
  0.0 591.6 jit_solution(10280611587841758913)
XLA Ops:
  8.0 24.8 %all-gather = bf16[16,2,8192]{2,1,0:T(2,128)(2,1)S(1)} all-gather(bf16[1,2,8192]{2,1,0:T(2,128)(2,1)} %bitcast.32), channel_id=1, replica_groups=mesh['group'=2,'shard'=16] {'shard'}, dimensions={0}, use_global_device_ids=true | all-gather | bytes 557056 | tf_op jit(solution)/shard_map/all_gather | solution.py:33
  33.7 6.7 %select_add_fusion = f32[512,4096]{1,0:T(8,128)} fusion(f32[512,4096]{1,0:T(8,128)} %param.7, f32[]{:T(128)} %bitcast.31, s32[4096]{0:T(1024)S(1)} %iota_add_fusion.1, s32[512]{0:T(512)S(1)} %iota_add_fusion.2, bf16[32,8192]{1,0:T(8,128)(2,1)S(1)} %reshape.41, s32[]{:T(128)S(6)} %select_n.180, s32[]{:T(128)S(6)} %select_n.179), kind=kOutput, calls=%fused_computation.29 | convolution fusion | flops 146800640 | bytes 17090572 | tf_op jit(solution)/shard_map/dot_general | solution.py:36
  40.4 345.1 %while.17 = (s32[]{:T(128)}, f32[512,4096]{1,0:T(8,128)}, s32[]{:T(128)}, s32[4096]{0:T(1024)S(1)}, s32[]{:T(128)}, /*index=5*/s32[]{:T(128)}, s32[]{:T(128)}, s...) while((s32[]{:T(128)}, f32[512,4096]{1,0:T(8,128)}, ...), condition=%wide.region_6.7_spmd.clone, body=%wide.region_0.6_spmd.clone.sunk | while | flops 4838440960 | bytes 54937316 | solution.py:70
  40.4 1.7 dynamic-slice_select_fusion.6
  42.2 3.1 dynamic-slice_select_fusion.7
  45.3 19.4 %all-reduce.6.cloned.1.call-done = f32[512,128]{1,0:T(8,128)} async-done(((f32[512,128]{1,0:T(8,128)}), f32[512,128]{1,0:T(8,128)}) %all-reduce.6.cloned.1.call-update) | async-done | bytes 262160 | tf_op jit(solution)/shard_map/while/body/eval_jaxpr/psum | solution.py:14
  64.6 1.5 dynamic-slice_select_fusion.8
  66.1 101.6 %all-reduce.8.cloned.1.call-done = (f32[128,4096]{1,0:T(8,128)}, f32[128,128]{1,0:T(8,128)}) async-done(((f32[128,4096]{1,0:T(8,128)}, f32[128,128]{1,0:T(8,128)}), (f32[128,4096]{1,0:T(8,128)}, f32[128,128]{1,0:T(8,128)})) %all-reduce.8.cloned.1.call-update) | async-done | bytes 2162704 | tf_op jit(solution)/shard_map/while/body/eval_jaxpr/psum | solution.py:14
  167.7 0.9 copy.9
  168.6 0.9 fusion.45
  169.5 11.7 %cholesky.59 = f32[128,128]{1,0:T(8,128)S(1)} custom-call(f32[128,128]{1,0:T(8,128)S(1)} %fusion.45), custom_call_target="Cholesky" | custom-call | tf_op jit(solution)/shard_map/while/body/eval_jaxpr/jit(cholesky)/cholesky | solution.py:18
  182.6 9.8 %custom-call.26 = f32[1,128,128]{1,2,0:T(8,128)S(1)} custom-call(f32[1,128,128]{2,1,0:T(8,128)S(1)} %fusion.46), custom_call_target="InvertDiagBlocksLowerTriangular" | custom-call | tf_op jit(solution)/shard_map/while/body/eval_jaxpr/triangular_solve | solution.py:20
  192.4 3.6 fusion.47
  196.0 1.9 fusion.48
  197.9 11.1 %convolution_subtract_fusion.2 = f32[512,4096]{1,0:T(8,128)} fusion(f32[512,4096]{1,0:T(8,128)} %get-tuple-element.225, f32[512,128]{1,0:T(8,128)S(1)} %copy-done, f32[128,4096]{1,0:T(8,128)S(1)} %fusion.48), kind=kOutput, calls=%fused_computation.2.clone.1 | convolution fusion | flops 3223322624 | bytes 19136512 | tf_op jit(solution)/shard_map/while/body/eval_jaxpr/dot_general | solution.py:63
  209.1 3.2 add_dynamic-update-slice_fusion.2
  212.3 1.7 dynamic-slice_select_fusion.6
  214.1 3.1 dynamic-slice_select_fusion.7
  217.2 20.8 %all-reduce.6.cloned.1.call-done = f32[512,128]{1,0:T(8,128)} async-done(((f32[512,128]{1,0:T(8,128)}), f32[512,128]{1,0:T(8,128)}) %all-reduce.6.cloned.1.call-update) | async-done | bytes 262160 | tf_op jit(solution)/shard_map/while/body/eval_jaxpr/psum | solution.py:14
  237.9 1.5 dynamic-slice_select_fusion.8
  239.4 101.5 %all-reduce.8.cloned.1.call-done = (f32[128,4096]{1,0:T(8,128)}, f32[128,128]{1,0:T(8,128)}) async-done(((f32[128,4096]{1,0:T(8,128)}, f32[128,128]{1,0:T(8,128)}), (f32[128,4096]{1,0:T(8,128)}, f32[128,128]{1,0:T(8,128)})) %all-reduce.8.cloned.1.call-update) | async-done | bytes 2162704 | tf_op jit(solution)/shard_map/while/body/eval_jaxpr/psum | solution.py:14
  340.9 0.9 copy.9
  342.7 11.7 %cholesky.59 = f32[128,128]{1,0:T(8,128)S(1)} custom-call(f32[128,128]{1,0:T(8,128)S(1)} %fusion.45), custom_call_target="Cholesky" | custom-call | tf_op jit(solution)/shard_map/while/body/eval_jaxpr/jit(cholesky)/cholesky | solution.py:18
  355.7 9.8 %custom-call.26 = f32[1,128,128]{1,2,0:T(8,128)S(1)} custom-call(f32[1,128,128]{2,1,0:T(8,128)S(1)} %fusion.46), custom_call_target="InvertDiagBlocksLowerTriangular" | custom-call | tf_op jit(solution)/shard_map/while/body/eval_jaxpr/triangular_solve | solution.py:20
  365.6 3.6 fusion.47
  369.2 1.9 fusion.48
  371.1 11.1 %convolution_subtract_fusion.2 = f32[512,4096]{1,0:T(8,128)} fusion(f32[512,4096]{1,0:T(8,128)} %get-tuple-element.225, f32[512,128]{1,0:T(8,128)S(1)} %copy-done, f32[128,4096]{1,0:T(8,128)S(1)} %fusion.48), kind=kOutput, calls=%fused_computation.2.clone.1 | convolution fusion | flops 3223322624 | bytes 19136512 | tf_op jit(solution)/shard_map/while/body/eval_jaxpr/dot_general | solution.py:63
  382.2 3.2 add_dynamic-update-slice_fusion.2
  386.1 126.8 %all-gather.3.cloned.1.call-done = bf16[2048,4096]{1,0:T(8,128)(2,1)} async-done(((bf16[128,4096]{1,0:T(8,128)(2,1)}), bf16[2048,4096]{1,0:T(8,128)(2,1)}) %all-gather.3.cloned.1.call-update) | async-done | bytes 16777232 | tf_op jit(solution)/shard_map/all_gather | solution.py:74
  512.9 16.2 %fusion.20 = f32[512,2048]{1,0:T(8,128)} fusion(bf16[2048,4096]{1,0:T(8,128)(2,1)} %all-gather.3.cloned.1.call-done, f32[512,4096]{1,0:T(8,128)} %get-tuple-element.154), kind=kOutput, calls=%fused_computation.30 | convolution fusion | flops 8592031744 | bytes 29360128 | tf_op jit(solution)/shard_map/dot_general | solution.py:72
  529.1 52.6 %reduce-scatter.2.cloned.1.call-done = f32[512,1024]{1,0:T(8,128)} async-done(((f32[512,2048]{1,0:T(8,128)}), f32[512,1024]{1,0:T(8,128)}) %reduce-scatter.2.cloned.1.call-update) | async-done | bytes 2097168 | tf_op jit(solution)/shard_map/reduce_scatter | solution.py:78
  581.7 2.7 convert_element_type.7
  (26 shorter events, 4.5 us)
Async XLA Ops:
  40.4 24.2 %all-reduce.6.cloned.1.call-start = ((), (), s32[]{:S(2)}) async-start(), calls=%async_computation.3 | async-start | bytes 524288 | tf_op jit(solution)/shard_map/while/body/eval_jaxpr/psum | solution.py:14
  42.1 125.6 %all-reduce.8.cloned.1.call-start = ((), (), s32[]{:S(2)}) async-start(), calls=%async_computation.4 | async-start | bytes 4325376 | tf_op jit(solution)/shard_map/while/body/eval_jaxpr/psum | solution.py:14
  192.4 5.6 copy-start
  212.3 25.6 %all-reduce.6.cloned.1.call-start = ((), (), s32[]{:S(2)}) async-start(), calls=%async_computation.3 | async-start | bytes 524288 | tf_op jit(solution)/shard_map/while/body/eval_jaxpr/psum | solution.py:14
  214.0 126.9 %all-reduce.8.cloned.1.call-start = ((), (), s32[]{:S(2)}) async-start(), calls=%async_computation.4 | async-start | bytes 4325376 | tf_op jit(solution)/shard_map/while/body/eval_jaxpr/psum | solution.py:14
  365.6 5.6 copy-start
  385.5 127.5 %all-gather.3.cloned.1.call-start = ((), (), s32[]{:S(2)}) async-start(), calls=%async_computation.1 | async-start | bytes 17825792 | tf_op jit(solution)/shard_map/all_gather | solution.py:74
  386.0 195.7 %reduce-scatter.2.cloned.1.call-start = ((), (), s32[]{:S(2)}) async-start(), calls=%async_computation.2 | async-start | bytes 6291456 | tf_op jit(solution)/shard_map/reduce_scatter | solution.py:78
Sparse Core Ops, SparseCore 0:
  44.0 20.5 all-reduce.5
  68.8 98.8 all-reduce.7
  215.9 21.9 all-reduce.5
  241.9 98.9 all-reduce.7
Sparse Core Ops, SparseCore 1:
  388.1 124.8 all-gather.2
  529.2 52.5 reduce-scatter.1
where the time goes:
time: 592 us
  waiting for transfers between devices  423 us (71%)
  other arithmetic  69.1 us (12%)
  matrix products  56.1 us (9%)
  blocking collectives  24.8 us (4%)
  between operations  15.8 us (3%)
    psum x4, waiting for transfers between devices, spread(): return lax.psum(block, axis)  243 us
    all_gather x1, waiting for transfers between devices, on_device(): lax.all_gather(gradients, 'shard', axis=0, tiled=True)  127 us
    reduce_scatter x1, waiting for transfers between devices, on_device(): lax.psum_scatter(partial_terms, 'group', scatter_dimension=1, tiled=True)  52.6 us
    all_gather x1, blocking collectives, on_device(): token_piece = lax.all_gather(samples, 'shard', axis=0, tiled=True)  24.8 us
    another operation x6, other arithmetic, solve_spd(): lower_factor = jnp.linalg.cholesky(pivot_block)  24.8 us
    dot_general x2, matrix products, sweep_once(): jnp.dot(column, factor_q, precision=lax.Precision.HIGHEST, preferred_elem...  22.2 us
    another operation x4, other arithmetic, solve_spd(): lax.linalg.triangular_solve(lower_factor, half_solved, left_side=True, lo...  20.9 us
    dot_general x1, matrix products, on_device(): lax.dot_general(swept_half, lax.all_gather(gradients, 'shard', axis=0, ti...  16.2 us
  transfers between devices with their start and end apart: 6, of which 6 were waited for; matrix products, arithmetic and copies ran while one was open for 1% of the time, Pallas kernels for 0%

commit v1 on v0

--- a/solution.py
+++ b/solution.py
@@ -11,7 +11,7 @@
 
 def spread(block, axis, holder):
     block = jnp.where(lax.axis_index(axis) == holder, block, jnp.zeros_like(block))
-    return lax.psum(block, axis)
+    return jnp.sum(lax.all_gather(block, axis), axis=0)
 
 
 def solve_spd(pivot_block, right_side):

time: 592 us -> 741 us (1.25)
  waiting for transfers between devices: 423 us -> 537 us
  other arithmetic: 69.1 us -> 90.5 us
  blocking collectives: 24.8 us -> 43.2 us
    all_gather x0 -> x4, waiting for transfers between devices: none -> 356 us  [spread(): return jnp.sum(lax.all_gather(block, axis), axis=0)]
    psum x4 -> x0, waiting for transfers between devices: 243 us -> none  [spread(): return lax.psum(block, axis)]
    reduce_sum x0 -> x6, other arithmetic: none -> 26.1 us  [spread(): return jnp.sum(lax.all_gather(block, axis), axis=0)]
    all_gather x0 -> x2, blocking collectives: none -> 18.4 us  [spread(): return jnp.sum(lax.all_gather(block, axis), axis=0)]
  transfers between devices with their start and end apart: 6 -> 6, of which waited for: 6 -> 6; matrix products, arithmetic and copies ran while one was open for 1% -> 7% of each run, Pallas kernels for 0% -> 0%
where the time goes in v1:
time: 741 us; the launch traced here: 740 us
  waiting for transfers between devices  537 us (72%)
  other arithmetic  90.5 us (12%)
  matrix products  52.9 us (7%)
  blocking collectives  43.2 us (6%)
  between operations  15.8 us (2%)
    all_gather x4, waiting for transfers between devices, spread(): return jnp.sum(lax.all_gather(block, axis), axis=0)  356 us
    all_gather x1, waiting for transfers between devices, on_device(): lax.all_gather(gradients, 'shard', axis=0, tiled=True)  128 us
    reduce_scatter x1, waiting for transfers between devices, on_device(): lax.psum_scatter(partial_terms, 'group', scatter_dimension=1, tiled=True)  52.6 us
    reduce_sum x6, other arithmetic, spread(): return jnp.sum(lax.all_gather(block, axis), axis=0)  26.1 us
    all_gather x1, blocking collectives, on_device(): token_piece = lax.all_gather(samples, 'shard', axis=0, tiled=True)  24.8 us
    another operation x6, other arithmetic, solve_spd(): lower_factor = jnp.linalg.cholesky(pivot_block)  24.8 us
    dot_general x2, matrix products, sweep_once(): jnp.dot(column, factor_q, precision=lax.Precision.HIGHEST, preferred_elem...  22.2 us
    another operation x4, other arithmetic, solve_spd(): lax.linalg.triangular_solve(lower_factor, half_solved, left_side=True, lo...  20.9 us
  transfers between devices with their start and end apart: 6, of which 6 were waited for; matrix products, arithmetic and copies ran while one was open for 7% of the time, Pallas kernels for 0%

profile of v1, /device:TPU:0, one launch (start us, length us, event | category | flops | bytes accessed | tf_op | source)
XLA Modules:
  0.0 740.0 jit_solution(3140730088160505185)
XLA Ops:
  8.7 24.8 %all-gather.3 = bf16[16,2,8192]{2,1,0:T(2,128)(2,1)S(1)} all-gather(bf16[1,2,8192]{2,1,0:T(2,128)(2,1)} %bitcast.44), channel_id=1, replica_groups=mesh['group'=2,'shard'=16] {'shard'}, dimensions={0}, use_global_device_ids=true | all-gather | bytes 557056 | tf_op jit(solution)/shard_map/all_gather | solution.py:33
  33.7 6.7 select_add_fusion
  40.4 492.2 %while.17 = (s32[]{:T(128)}, f32[512,4096]{1,0:T(8,128)}, s32[]{:T(128)}, s32[4096]{0:T(1024)S(1)}, s32[]{:T(128)}, /*index=5*/s32[]{:T(128)}, s32[]{:T(128)}, s...) while((s32[]{:T(128)}, f32[512,4096]{1,0:T(8,128)}, ...), condition=%wide.region_6.7_spmd.clone, body=%wide.region_0.6_spmd.clone.sunk | while | flops 4846010368 | bytes 187975376 | solution.py:70
  40.4 1.0 dynamic-slice_select_fusion.6
  41.3 9.2 %all-gather.10 = f32[1024,128]{1,0:T(8,128)S(1)} all-gather(f32[512,128]{1,0:T(8,128)S(1)} %dynamic-slice_select_fusion.6), channel_id=2, replica_groups=mesh['group'=2,'shard'=16] {'group'}, dimensions={0}, use_global_device_ids=true | all-gather | bytes 786432 | tf_op jit(solution)/shard_map/while/body/eval_jaxpr/all_gather | solution.py:14
  51.3 3.1 dynamic-slice_select_fusion.7
  54.5 32.1 %all-gather.21.cloned.1.call-done = f32[2048,128]{1,0:T(8,128)} async-done(((f32[128,128]{1,0:T(8,128)}), f32[2048,128]{1,0:T(8,128)}) %all-gather.21.cloned.1.call-update) | async-done | bytes 1048592 | tf_op jit(solution)/shard_map/while/body/eval_jaxpr/all_gather | solution.py:14
  86.5 1.3 reduce_sum.59
  88.0 11.7 %cholesky.59 = f32[128,128]{1,0:T(8,128)S(1)} custom-call(f32[128,128]{1,0:T(8,128)S(1)} %fusion.45), custom_call_target="Cholesky" | custom-call | tf_op jit(solution)/shard_map/while/body/eval_jaxpr/jit(cholesky)/cholesky | solution.py:18
  101.0 9.8 %custom-call.26 = f32[1,128,128]{1,2,0:T(8,128)S(1)} custom-call(f32[1,128,128]{2,1,0:T(8,128)S(1)} %fusion.46), custom_call_target="InvertDiagBlocksLowerTriangular" | custom-call | tf_op jit(solution)/shard_map/while/body/eval_jaxpr/triangular_solve | solution.py:20
  110.8 144.5 %all-gather.19.cloned.1.call-done = f32[2048,4096]{1,0:T(8,128)} async-done(((f32[128,4096]{1,0:T(8,128)}), f32[2048,4096]{1,0:T(8,128)}) %all-gather.19.cloned.1.call-update) | async-done | bytes 33554448 | tf_op jit(solution)/shard_map/while/body/eval_jaxpr/all_gather | solution.py:14
  255.3 11.8 %reduce_sum.58 = f32[128,4096]{1,0:T(8,128)S(1)} reduce(f32[16,128,4096]{2,1,0:T(8,128)} %bitcast.41, f32[]{:T(128)} %constant.236.clone.12..sunk), dimensions={0}, to_apply=%region_5.5 | reduce | flops 7864320 | bytes 35651588 | tf_op jit(solution)/shard_map/while/body/eval_jaxpr/reduce_sum | solution.py:14
  267.0 2.0 fusion.47
  269.1 1.9 fusion.48
  271.0 11.1 %convolution_subtract_fusion.2 = f32[512,4096]{1,0:T(8,128)} fusion(f32[512,4096]{1,0:T(8,128)} %get-tuple-element.220, f32[512,128]{1,0:T(8,128)S(1)} %reduce_sum.57, f32[128,4096]{1,0:T(8,128)S(1)} %fusion.48), kind=kOutput, calls=%fused_computation.2.clone.1 | convolution fusion | flops 3223322624 | bytes 19136512 | tf_op jit(solution)/shard_map/while/body/eval_jaxpr/dot_general | solution.py:63
  282.1 3.2 add_dynamic-update-slice_fusion.2
  286.3 9.1 %all-gather.10 = f32[1024,128]{1,0:T(8,128)S(1)} all-gather(f32[512,128]{1,0:T(8,128)S(1)} %dynamic-slice_select_fusion.6), channel_id=2, replica_groups=mesh['group'=2,'shard'=16] {'group'}, dimensions={0}, use_global_device_ids=true | all-gather | bytes 786432 | tf_op jit(solution)/shard_map/while/body/eval_jaxpr/all_gather | solution.py:14
  296.2 3.1 dynamic-slice_select_fusion.7
  299.3 34.7 %all-gather.21.cloned.1.call-done = f32[2048,128]{1,0:T(8,128)} async-done(((f32[128,128]{1,0:T(8,128)}), f32[2048,128]{1,0:T(8,128)}) %all-gather.21.cloned.1.call-update) | async-done | bytes 1048592 | tf_op jit(solution)/shard_map/while/body/eval_jaxpr/all_gather | solution.py:14
  334.0 1.3 reduce_sum.59
  335.4 11.7 %cholesky.59 = f32[128,128]{1,0:T(8,128)S(1)} custom-call(f32[128,128]{1,0:T(8,128)S(1)} %fusion.45), custom_call_target="Cholesky" | custom-call | tf_op jit(solution)/shard_map/while/body/eval_jaxpr/jit(cholesky)/cholesky | solution.py:18
  348.5 9.8 %custom-call.26 = f32[1,128,128]{1,2,0:T(8,128)S(1)} custom-call(f32[1,128,128]{2,1,0:T(8,128)S(1)} %fusion.46), custom_call_target="InvertDiagBlocksLowerTriangular" | custom-call | tf_op jit(solution)/shard_map/while/body/eval_jaxpr/triangular_solve | solution.py:20
  358.3 144.3 %all-gather.19.cloned.1.call-done = f32[2048,4096]{1,0:T(8,128)} async-done(((f32[128,4096]{1,0:T(8,128)}), f32[2048,4096]{1,0:T(8,128)}) %all-gather.19.cloned.1.call-update) | async-done | bytes 33554448 | tf_op jit(solution)/shard_map/while/body/eval_jaxpr/all_gather | solution.py:14
  502.6 11.8 %reduce_sum.58 = f32[128,4096]{1,0:T(8,128)S(1)} reduce(f32[16,128,4096]{2,1,0:T(8,128)} %bitcast.41, f32[]{:T(128)} %constant.236.clone.12..sunk), dimensions={0}, to_apply=%region_5.5 | reduce | flops 7864320 | bytes 35651588 | tf_op jit(solution)/shard_map/while/body/eval_jaxpr/reduce_sum | solution.py:14
  514.3 2.0 fusion.47
  516.3 1.9 fusion.48
  518.2 11.1 %convolution_subtract_fusion.2 = f32[512,4096]{1,0:T(8,128)} fusion(f32[512,4096]{1,0:T(8,128)} %get-tuple-element.220, f32[512,128]{1,0:T(8,128)S(1)} %reduce_sum.57, f32[128,4096]{1,0:T(8,128)S(1)} %fusion.48), kind=kOutput, calls=%fused_computation.2.clone.1 | convolution fusion | flops 3223322624 | bytes 19136512 | tf_op jit(solution)/shard_map/while/body/eval_jaxpr/dot_general | solution.py:63
  529.4 3.2 add_dynamic-update-slice_fusion.2
  533.2 128.2 %all-gather.17.cloned.1.call-done = bf16[2048,4096]{1,0:T(8,128)(2,1)} async-done(((bf16[128,4096]{1,0:T(8,128)(2,1)}), bf16[2048,4096]{1,0:T(8,128)(2,1)}) %all-gather.17.cloned.1.call-update) | async-done | bytes 16777232 | tf_op jit(solution)/shard_map/all_gather | solution.py:74
  661.4 16.2 %fusion.20 = f32[512,2048]{1,0:T(8,128)} fusion(bf16[2048,4096]{1,0:T(8,128)(2,1)} %all-gather.17.cloned.1.call-done, f32[512,4096]{1,0:T(8,128)} %get-tuple-element.154), kind=kOutput, calls=%fused_computation.30 | convolution fusion | flops 8592031744 | bytes 29360128 | tf_op jit(solution)/shard_map/dot_general | solution.py:72
  677.6 52.6 %reduce-scatter.2.cloned.1.call-done = f32[512,1024]{1,0:T(8,128)} async-done(((f32[512,2048]{1,0:T(8,128)}), f32[512,1024]{1,0:T(8,128)}) %reduce-scatter.2.cloned.1.call-update) | async-done | bytes 2097168 | tf_op jit(solution)/shard_map/reduce_scatter | solution.py:78
  730.2 2.7 convert_element_type.7
  (30 shorter events, 6.2 us)
Async XLA Ops:
  40.4 46.2 %all-gather.21.cloned.1.call-start = ((), (), s32[]{:S(2)}) async-start(), calls=%async_computation.4 | async-start | bytes 1114112 | tf_op jit(solution)/shard_map/while/body/eval_jaxpr/all_gather | solution.py:14
  51.3 204.0 %all-gather.19.cloned.1.call-start = ((), (), s32[]{:S(2)}) async-start(), calls=%async_computation.3 | async-start | bytes 35651584 | tf_op jit(solution)/shard_map/while/body/eval_jaxpr/all_gather | solution.py:14
  285.3 48.7 %all-gather.21.cloned.1.call-start = ((), (), s32[]{:S(2)}) async-start(), calls=%async_computation.4 | async-start | bytes 1114112 | tf_op jit(solution)/shard_map/while/body/eval_jaxpr/all_gather | solution.py:14
  296.1 206.5 %all-gather.19.cloned.1.call-start = ((), (), s32[]{:S(2)}) async-start(), calls=%async_computation.3 | async-start | bytes 35651584 | tf_op jit(solution)/shard_map/while/body/eval_jaxpr/all_gather | solution.py:14
  532.6 128.8 %all-gather.17.cloned.1.call-start = ((), (), s32[]{:S(2)}) async-start(), calls=%async_computation.1 | async-start | bytes 17825792 | tf_op jit(solution)/shard_map/all_gather | solution.py:74
  533.1 197.0 %reduce-scatter.2.cloned.1.call-start = ((), (), s32[]{:S(2)}) async-start(), calls=%async_computation.2 | async-start | bytes 6291456 | tf_op jit(solution)/shard_map/reduce_scatter | solution.py:78
Sparse Core Ops, SparseCore 0:
  51.4 35.1 all-gather.20
  88.1 167.0 all-gather.18
  296.2 37.7 all-gather.20
  335.5 167.0 all-gather.18
Sparse Core Ops, SparseCore 1:
  535.2 126.1 all-gather.16
  677.6 52.5 reduce-scatter.1
